TPU v7x, 32 devices: a whole 2x2x4 slice. The times are simulated.
32 devices in a mesh: seq: 4 (over y, x), feat: 8 (over z, core).
Axes of the slice: x: 2, y: 2, z: 4, core: 2. Of those that a mesh axis runs over, the one named last changes fastest.
Arguments:
- queries: bfloat16 [3840, 16, 128], P('seq'), may hold values from -32 to 32
- key_vectors: bfloat16 [3840, 16, 128], P('seq'), may hold values from -32 to 32
- values: bfloat16 [3840, 16, 128], P('seq'), may hold values from -6 to 6
- projections: bfloat16 [16, 4096, 128], P(None, 'feat'), may hold values from -4 to 4
Outputs:
- attended: bfloat16 [3840, 16, 128], P('seq', 'feat')
All inputs are finite; a program needn't handle non-finite values.
Results may differ from a plain program's by a relative error of at most 0.012.
Values may be sent and summed in bfloat16 or wider, within the bound.
A program may use at most 128 MiB of HBM per device.

v0:
```python
import jax
import jax.numpy as jnp
from jax import lax
from jax.sharding import PartitionSpec as P

E = 128


def key_exponents(key_vectors, directions, scaling):
    key_dash = (
        jnp.einsum("the,hme->thm", key_vectors, directions, preferred_element_type=jnp.float32)
        * scaling
    )
    key_diag = jnp.sum(jnp.square(key_vectors.astype(jnp.float32)), axis=2) * (
        0.5 * scaling * scaling
    )
    return key_dash - key_diag[:, :, None]


def key_terms(key_expo, key_peak, values):
    key_phi = jnp.exp(key_expo - key_peak[None, :, None]).astype(jnp.bfloat16)
    key_state = jnp.einsum("thm,the->hme", key_phi, values, preferred_element_type=jnp.float32)
    key_mass = jnp.sum(key_phi, axis=0, dtype=jnp.float32)
    return (key_state, key_mass)


def partial_output(query_dash, query_peak, state_half, key_mass):
    query_phi = jnp.exp(query_dash - query_peak[:, :, None]).astype(jnp.bfloat16)
    numerator = jnp.einsum(
        "thm,hme->the", query_phi, state_half, preferred_element_type=jnp.float32
    )
    denominator = jnp.einsum(
        "thm,hm->th", query_phi.astype(jnp.float32), key_mass, precision=lax.Precision.HIGHEST
    )
    return (numerator, denominator)


def shards(queries, key_vectors, values, projections):
    scaling = E ** (-0.25)
    directions = lax.all_to_all(projections, "feat", split_axis=0, concat_axis=1, tiled=True)
    head_share = queries.shape[1] // lax.axis_size("feat")
    start_head = lax.axis_index("feat") * head_share
    own_queries = lax.dynamic_slice_in_dim(queries, start_head, head_share, 1)
    own_keys = lax.dynamic_slice_in_dim(key_vectors, start_head, head_share, 1)
    own_values = lax.dynamic_slice_in_dim(values, start_head, head_share, 1)
    key_expo = key_exponents(own_keys, directions, scaling)
    key_peak = lax.pmax(jnp.max(key_expo, axis=(0, 2)), "seq")
    key_state, key_mass = key_terms(key_expo, key_peak, own_values)
    key_state, key_mass = lax.psum((key_state, key_mass), "seq")
    state_half = key_state.astype(jnp.bfloat16)
    query_dash = (
        jnp.einsum("the,hme->thm", own_queries, directions, preferred_element_type=jnp.float32)
        * scaling
    )
    numerator, denominator = partial_output(
        query_dash, jnp.max(query_dash, axis=2), state_half, key_mass
    )
    return (numerator / denominator[:, :, None]).astype(jnp.bfloat16)


def solution(mesh):
    placed = (
        P("seq", None, None),
        P("seq", None, None),
        P("seq", None, None),
        P(None, "feat", None),
    )
    return jax.shard_map(
        shards, mesh=mesh, in_specs=placed, out_specs=P("seq", "feat", None), check_vma=False
    )
```

profile of v0, /device:TPU:0, one launch (start us, length us, event | category | flops | bytes accessed | tf_op | source)
XLA Modules:
  0.0 290.5 jit_solution(13360563966676854355)
XLA Ops:
  0.0 6.4 %all-to-all-start = ((bf16[16,512,128]{2,1,0:T(8,128)(2,1)}), bf16[16,512,128]{2,1,0:T(8,128)(2,1)S(1)}, u32[]{:S(2)}, u32[]{:S(2)}) async-start(bf16[16,512,128]{2,1,0:T(8,128)(2,1)} %param.7), calls=%async_computation | async-start | bytes 4194304 | tf_op jit(solution)/shard_map/all_to_all | solution.py:40
  6.4 2.1 constant_dynamic-slice_fusion.2
  8.4 2.8 constant_dynamic-slice_fusion.1
  11.2 2.1 constant_dynamic-slice_fusion
  13.3 0.4 multiply_reduce_fusion
  13.7 41.7 %all-to-all-done = bf16[16,512,128]{2,1,0:T(8,128)(2,1)S(1)} async-done(((bf16[16,512,128]{2,1,0:T(8,128)(2,1)}), bf16[16,512,128]{2,1,0:T(8,128)(2,1)S(1)}, u32[]{:S(2)}, u32[]{:S(2)}) %all-to-all-start) | async-done | bytes 2097184 | tf_op jit(solution)/shard_map/all_to_all | solution.py:40
  55.4 0.0 copy-start
  55.4 1.3 copy-done
  56.7 1.7 copy.6
  58.5 12.5 %fusion.2 = (f32[2]{0:T(128)S(1)}, f32[2,960,4096]{2,1,0:T(8,128)}) fusion(f32[960,2]{0,1:T(2,128)S(1)} %broadcast_multiply_fusion, bf16[2,4096,128]{2,1,0:T(8,128)(2,1)S(1)} %bitcast.42, bf16[960,2,128]{2,1,0:T(2,128)(2,1)S(1)} %constant_dynamic-slice_fusion.2), kind=kOutput, calls=%fused_computation.7 | convolution fusion | flops 2036858880 | bytes 34053640 | tf_op jit(solution)/shard_map/the,hme->thm/dot_general | solution.py:11
  71.0 0.0 copy-start.1
  71.0 10.2 %pmax.7 = f32[2]{0:T(128)S(1)} all-reduce(f32[2]{0:T(128)S(1)} %get-tuple-element.9), channel_id=1, replica_groups=mesh['seq'=4,'feat'=8] {'seq'}, use_global_device_ids=true, to_apply=%region_2.0 | all-reduce | flops 2 | bytes 16 | tf_op jit(solution)/shard_map/pmax | solution.py:47
  81.1 14.1 %convert_reduce_fusion = (f32[2,4096]{1,0:T(2,128)S(1)}, bf16[960,2,4096]{2,0,1:T(8,128)(2,1)S(1)}) fusion(f32[2]{0:T(128)S(1)} %pmax.7, f32[960,2]{0,1:T(2,128)S(1)} %broadcast_multiply_fusion, f32[2,960,4096]{2,1,0:T(8,128)} %get-tuple-element.10), kind=kLoop, calls=%fused_computation.5 | loop fusion | flops 47177728 | bytes 47226376 | tf_op jit(solution)/shard_map/reduce_sum | solution.py:23
  95.3 0.0 copy-done.1
  95.3 8.3 %fusion.25 = f32[2,4096,128]{2,1,0:T(8,128)} fusion(bf16[960,2,4096]{2,0,1:T(8,128)(2,1)S(1)} %get-tuple-element.8, bf16[960,2,128]{2,1,0:T(2,128)(2,1)S(1)} %copy-done.1), kind=kOutput, calls=%fused_computation.17 | convolution fusion | flops 2013265920 | bytes 20414464 | tf_op jit(solution)/shard_map/thm,the->hme/dot_general | solution.py:22
  103.6 12.4 %bitcast_reduce_fusion = (f32[960,2]{0,1:T(2,128)S(1)}, f32[2,960,4096]{2,1,0:T(8,128)}) fusion(bf16[2,4096,128]{2,1,0:T(8,128)(2,1)S(1)} %bitcast.43, bf16[960,2,128]{2,1,0:T(2,128)(2,1)S(1)} %constant_dynamic-slice_fusion), kind=kOutput, calls=%fused_computation.1 | convolution fusion | flops 2028992640 | bytes 34053632 | tf_op jit(solution)/shard_map/the,hme->thm/dot_general | solution.py:52
  116.0 142.1 %all-reduce.2 = (bf16[2,4096,128]{2,1,0:T(8,128)(2,1)S(1)}, f32[2,4096]{1,0:T(2,128)S(1)}) all-reduce(f32[2,4096,128]{2,1,0:T(8,128)} %fusion.25, f32[2,4096]{1,0:T(2,128)S(1)} %get-tuple-element.7), channel_id=1, replica_groups=mesh['seq'=4,'feat'=8] {'seq'}, use_global_device_ids=true, to_apply=%region_3.0 | all-reduce | flops 1056768 | bytes 6356992 | tf_op jit(solution)/shard_map/psum | solution.py:49
  258.1 18.6 %fusion.3 = f32[2,1,960]{2,1,0:T(1,128)S(1)} fusion(f32[2,960,4096]{2,1,0:T(8,128)} %get-tuple-element.12, f32[960,2]{0,1:T(2,128)S(1)} %get-tuple-element.11, f32[2,4096,1]{1,0,2:T(2,128)S(1)} %bitcast.45), kind=kOutput, calls=%fused_computation.8 | convolution fusion | flops 117964800 | bytes 31505408 | tf_op jit(solution)/shard_map/thm,hm->th/dot_general | solution.py:32
  276.7 12.5 %fusion.18 = bf16[960,2,128]{2,0,1:T(8,128)(2,1)S(1)} fusion(bf16[2,4096,128]{2,1,0:T(8,128)(2,1)S(1)} %get-tuple-element.5, f32[2,960,4096]{2,1,0:T(8,128)} %get-tuple-element.12, f32[960,2]{0,1:T(2,128)S(1)} %get-tuple-element.11, f32[960,2]{0,1:T(2,128)S(1)} %bitcast.46), kind=kOutput, calls=%fused_computation.13 | convolution fusion | flops 2037350400 | bytes 34061312 | tf_op jit(solution)/shard_map/thm,hme->the/dot_general | solution.py:29
  289.2 1.3 copy.8
  (2 shorter events, 0.0 us)
Async XLA Ops:
  0.0 55.4 %all-to-all-start = ((bf16[16,512,128]{2,1,0:T(8,128)(2,1)}), bf16[16,512,128]{2,1,0:T(8,128)(2,1)S(1)}, u32[]{:S(2)}, u32[]{:S(2)}) async-start(bf16[16,512,128]{2,1,0:T(8,128)(2,1)} %param.7), calls=%async_computation | async-start | bytes 4194304 | tf_op jit(solution)/shard_map/all_to_all | solution.py:40
  55.4 1.4 copy-start
  71.0 24.3 %copy-start.1 = (bf16[960,2,128]{2,1,0:T(2,128)(2,1)S(1)}, bf16[960,2,128]{2,1,0:T(2,128)(2,1)}, u32[]{:S(2)}) copy-start(bf16[960,2,128]{2,1,0:T(2,128)(2,1)} %constant_dynamic-slice_fusion.1) | copy-start | bytes 1474564
where the time goes:
time: 291 us
  blocking collectives  152 us (52%)
  matrix products  64.3 us (22%)
  waiting for transfers between devices  41.7 us (14%)
  other arithmetic  14.5 us (5%)
  local copies, waits for them, and re-layouts  11.3 us (4%)
  starting transfers between devices  6.35 us (2%)
    psum x1, blocking collectives, shards(): key_state, key_mass = lax.psum((key_state, key_mass), 'seq')  142 us
    all_to_all x1, waiting for transfers between devices, shards(): lax.all_to_all(projections, 'feat', split_axis=0, concat_axis=1, tiled=True)  41.7 us
    dot_general x1, matrix products, partial_output(): jnp.einsum('thm,hm->th', query_phi.astype(jnp.float32), key_mass, precisi...  18.6 us
    reduce_sum x1, other arithmetic, key_terms(): key_mass = jnp.sum(key_phi, axis=0, dtype=jnp.float32)  14.1 us
    dot_general x1, matrix products, partial_output(): jnp.einsum('thm,hme->the', query_phi, state_half, preferred_element_type=...  12.5 us
    dot_general x1, matrix products, key_exponents(): jnp.einsum('the,hme->thm', key_vectors, directions, preferred_element_typ...  12.5 us
    dot_general x1, matrix products, shards(): jnp.einsum('the,hme->thm', own_queries, directions, preferred_element_typ...  12.4 us
    pmax x1, blocking collectives, shards(): key_peak = lax.pmax(jnp.max(key_expo, axis=(0, 2)), 'seq')  10.2 us
  transfers between devices with their start and end apart: 1, of which 1 were waited for; matrix products, arithmetic and copies ran while one was open for 3% of the time, Pallas kernels for 0%

commit v1 on v0

--- a/solution.py
+++ b/solution.py
@@ -1,9 +1,16 @@
+import functools
+import math
+
 import jax
 import jax.numpy as jnp
 from jax import lax
+from jax.experimental import pallas as pl
+from jax.experimental.pallas import tpu as pltpu
 from jax.sharding import PartitionSpec as P
 
 E = 128
+AHEAD = 2
+BEHIND = 1
 
 
 def key_exponents(key_vectors, directions, scaling):
@@ -58,6 +65,273 @@
     return (numerator / denominator[:, :, None]).astype(jnp.bfloat16)
 
 
+MESH = pl.DeviceIdType.MESH
+LOW = -1e30
+
+
+def dot_nt(a, b):
+    return lax.dot_general(a, b, (((1,), (1,)), ((), ())), preferred_element_type=jnp.float32)
+
+
+def flip(index, bits, width):
+    out = index
+    bit = 1
+    while bit < width:
+        if bits & bit:
+            out = out + bit * (1 - 2 * ((index // bit) % 2))
+        bit *= 2
+    return out
+
+
+def head_kernel(
+    chunks, ahead, behind, scale,
+    q_hbm, k_hbm, v_hbm, dirs_hbm, out_ref,
+    q_ref, k_ref, v_ref, diag_ref, w_ref,
+    state_ref, peak_ref, send_ref, recv_ref, send_aux, recv_aux,
+    acc_ref, row_ref, top_ref, result_ref,
+    load_sem, x_send, x_recv, w_send, w_recv, y_send, y_recv, o_send, o_recv,
+):
+    tokens, size = k_ref.shape[1:]
+    width = w_ref.shape[1]
+    groups = width // size
+    seq = lax.axis_index("seq")
+    feat = lax.axis_index("feat")
+    side = seq % 2
+    x_mate = flip(seq, 1, 4)
+    y_mate = flip(seq, 2, 4)
+    mates = [flip(feat, bits, chunks) for bits in range(1, chunks)]
+
+    own_loads = [
+        pltpu.make_async_copy(k_hbm.at[side], k_ref.at[0], load_sem.at[0]),
+        pltpu.make_async_copy(v_hbm.at[side], v_ref.at[0], load_sem.at[1]),
+        pltpu.make_async_copy(q_hbm.at[side], q_ref.at[0], load_sem.at[2]),
+        pltpu.make_async_copy(dirs_hbm.at[feat * 2 + side], w_ref.at[0], w_recv.at[0]),
+    ]
+    for load in own_loads:
+        load.start()
+
+    barrier = pltpu.get_barrier_semaphore()
+    pl.semaphore_signal(barrier, inc=1, device_id={"seq": x_mate}, device_id_type=MESH)
+    pl.semaphore_signal(barrier, inc=1, device_id={"seq": y_mate}, device_id_type=MESH)
+    for mate in mates:
+        pl.semaphore_signal(barrier, inc=1, device_id={"feat": mate}, device_id_type=MESH)
+    pl.semaphore_wait(barrier, 1 + chunks)
+
+    x_copies = []
+    for i, (src, dst) in enumerate(((k_hbm, k_ref), (v_hbm, v_ref), (q_hbm, q_ref))):
+        x_copies.append(pltpu.make_async_remote_copy(
+            src_ref=src.at[1 - side], dst_ref=dst.at[1],
+            send_sem=x_send.at[i], recv_sem=x_recv.at[i],
+            device_id={"seq": x_mate}, device_id_type=MESH))
+    w_copies = []
+    for i, mate in enumerate(mates):
+        w_copies.append(pltpu.make_async_remote_copy(
+            src_ref=dirs_hbm.at[mate * 2 + side], dst_ref=w_ref.at[i + 1],
+            send_sem=w_send.at[i + 1], recv_sem=w_recv.at[i + 1],
+            device_id={"feat": mate}, device_id_type=MESH))
+    for copy in x_copies[:2] + w_copies + x_copies[2:]:
+        copy.start()
+
+    def state_copies(slot):
+        return [
+            pltpu.make_async_remote_copy(
+                src_ref=send_ref.at[slot], dst_ref=recv_ref.at[slot],
+                send_sem=y_send.at[0, slot], recv_sem=y_recv.at[0, slot],
+                device_id={"seq": y_mate}, device_id_type=MESH),
+            pltpu.make_async_remote_copy(
+                src_ref=send_aux.at[slot], dst_ref=recv_aux.at[slot],
+                send_sem=y_send.at[1, slot], recv_sem=y_recv.at[1, slot],
+                device_id={"seq": y_mate}, device_id_type=MESH),
+        ]
+
+    acc_ref[...] = jnp.zeros_like(acc_ref)
+    row_ref[...] = jnp.full_like(row_ref, LOW)
+    top_ref[...] = jnp.full_like(top_ref, LOW)
+
+    lane_t = lax.broadcasted_iota(jnp.int32, (tokens, size), 1)
+    lane_w = lax.broadcasted_iota(jnp.int32, (width, size), 1)
+    minus = jnp.where(lane_w < 3, -1.0, 0.0).astype(jnp.bfloat16)
+    ones = jnp.ones((16, tokens), jnp.bfloat16)
+
+    def make_diag(half):
+        key = k_ref[half].astype(jnp.float32)
+        full = jnp.sum(key * key, axis=1, keepdims=True) * (0.5 * scale)
+        high = full.astype(jnp.bfloat16).astype(jnp.float32)
+        rest = full - high
+        mid = rest.astype(jnp.bfloat16).astype(jnp.float32)
+        low = rest - mid
+        block = jnp.where(lane_t == 0, high, jnp.where(lane_t == 1, mid, jnp.where(lane_t == 2, low, 0.0)))
+        diag_ref[half] = block.astype(jnp.bfloat16)
+
+    slope = scale * math.log2(math.e)
+
+    def key_unit(half, slot):
+        keys = jnp.concatenate([k_ref[half], diag_ref[half]], axis=1)
+        dirs = jnp.concatenate([w_ref[slot], minus], axis=1)
+        raw = dot_nt(keys, dirs)
+        peak = jnp.max(raw, axis=0, keepdims=True)
+        if half == 1:
+            before = peak_ref[slot, 0:1, :]
+            peak = jnp.maximum(peak, before)
+        phi = jnp.exp2((raw - peak) * slope).astype(jnp.bfloat16)
+        vals = jnp.concatenate([v_ref[half], ones], axis=0)
+        state = jnp.dot(vals, phi, preferred_element_type=jnp.float32)
+        if half == 1:
+            state = state + state_ref[slot] * jnp.exp2((before - peak) * slope)
+        state_ref[slot] = state
+        peak_ref[slot, 0:1, :] = peak
+        if half == 1:
+            send_ref[slot] = state[:size].astype(jnp.bfloat16)
+            for g in range(groups):
+                cut = slice(g * size, (g + 1) * size)
+                send_aux[slot, g:g + 1, :] = state[size:size + 1, cut]
+                send_aux[slot, groups + g:groups + g + 1, :] = peak[:, cut]
+
+    def query_unit(slot):
+        own_peak = peak_ref[slot, 0:1, :]
+        got_peak = jnp.concatenate([recv_aux[slot, groups + g:groups + g + 1, :] for g in range(groups)], axis=1)
+        got_mass = jnp.concatenate([recv_aux[slot, g:g + 1, :] for g in range(groups)], axis=1)
+        before = top_ref[0:1, 0:1]
+        top = jnp.maximum(before, jnp.max(jnp.maximum(own_peak, got_peak), axis=1, keepdims=True))
+        top_ref[...] = jnp.broadcast_to(top, top_ref.shape)
+        own_gain = jnp.exp2((own_peak - top) * slope)
+        got_gain = jnp.exp2((got_peak - top) * slope)
+        state = (state_ref[slot, 0:size, :] * own_gain + recv_ref[slot].astype(jnp.float32) * got_gain).astype(jnp.bfloat16)
+        mass = state_ref[slot, size:size + 1, :] * own_gain + got_mass * got_gain
+        high = mass.astype(jnp.bfloat16).astype(jnp.float32)
+        table = jnp.concatenate([
+            state,
+            jnp.broadcast_to(high, (size // 2, width)).astype(jnp.bfloat16),
+            jnp.broadcast_to(mass - high, (size // 2, width)).astype(jnp.bfloat16)], axis=0)
+        drop = (before - top) * slope
+
+        def one_half(half, carry):
+            raw = dot_nt(q_ref[half], w_ref[slot])
+            last = row_ref[half]
+            peak = jnp.maximum(last, jnp.max(raw, axis=1, keepdims=True))
+            row_ref[half] = peak
+            wide = jnp.concatenate([peak] * groups, axis=1)
+            phi = jnp.exp2((raw - wide) * slope).astype(jnp.bfloat16)
+            part = dot_nt(phi, table)
+            fade = jnp.exp2((last - peak) * slope + drop)
+            acc_ref[half] = acc_ref[half] * jnp.concatenate([fade, fade], axis=1) + part
+            return carry
+
+        lax.fori_loop(0, 2, one_half, 0)
+
+    def finish(half):
+        numer = acc_ref[half, :, 0:size]
+        denom = acc_ref[half, :, size:2 * size]
+        denom = denom + pltpu.roll(denom, size // 2, 1)
+        return (numer / denom).astype(jnp.bfloat16)
+
+    def step(t, carry):
+        @pl.when(t < chunks)
+        def _():
+            pltpu.make_async_copy(w_ref.at[t], w_ref.at[t], w_recv.at[t]).wait()
+            key_unit(0, t)
+
+        @pl.when(t == ahead)
+        def _():
+            x_copies[0].wait_recv()
+            x_copies[1].wait_recv()
+            make_diag(1)
+
+        @pl.when((t >= ahead) & (t < ahead + chunks))
+        def _():
+            key_unit(1, t - ahead)
+            for copy in state_copies(t - ahead):
+                copy.start()
+
+        @pl.when(t == ahead + behind)
+        def _():
+            own_loads[2].wait()
+            x_copies[2].wait_recv()
+
+        @pl.when(t >= ahead + behind)
+        def _():
+            slot = t - ahead - behind
+            for copy in state_copies(slot):
+                copy.wait_recv()
+            query_unit(slot)
+
+        return carry
+
+    own_loads[0].wait()
+    own_loads[1].wait()
+    make_diag(0)
+    lax.fori_loop(0, chunks + ahead + behind, step, 0)
+
+    result_ref[...] = finish(1)
+    out_copy = pltpu.make_async_remote_copy(
+        src_ref=result_ref, dst_ref=out_ref.at[side], send_sem=o_send, recv_sem=o_recv,
+        device_id={"seq": x_mate}, device_id_type=MESH)
+    out_copy.start()
+    out_ref[side] = finish(0)
+    for copy in x_copies:
+        copy.wait_send()
+    for copy in w_copies:
+        copy.wait_send()
+
+    def drain(t, carry):
+        for copy in state_copies(t):
+            copy.wait_send()
+        return carry
+
+    lax.fori_loop(0, chunks, drain, 0)
+    out_copy.wait()
+
+
+def paired_shards(chunks, queries, key_vectors, values, projections):
+    tokens, _, size = queries.shape
+    width = projections.shape[1]
+    scale = size ** -0.25
+    start = lax.axis_index("feat") * 2
+    pair = [lax.dynamic_slice_in_dim(a, start, 2, 1) for a in (queries, key_vectors, values)]
+    own_q, own_k = (jnp.transpose(a, (1, 0, 2)) for a in pair[:2])
+    own_v = jnp.transpose(pair[2], (1, 2, 0))
+    bf16, f32 = jnp.bfloat16, jnp.float32
+    dma = pltpu.SemaphoreType.DMA
+    out = pl.pallas_call(
+        functools.partial(head_kernel, chunks, AHEAD, BEHIND, scale),
+        out_shape=jax.ShapeDtypeStruct((2, tokens, size), bf16),
+        in_specs=[pl.BlockSpec(memory_space=pl.ANY)] * 4,
+        out_specs=pl.BlockSpec(memory_space=pltpu.VMEM),
+        scratch_shapes=[
+            pltpu.VMEM((2, tokens, size), bf16),
+            pltpu.VMEM((2, tokens, size), bf16),
+            pltpu.VMEM((2, size, tokens), bf16),
+            pltpu.VMEM((2, tokens, size), bf16),
+            pltpu.VMEM((chunks, width, size), bf16),
+            pltpu.VMEM((chunks, size + 16, width), f32),
+            pltpu.VMEM((chunks, 8, width), f32),
+            pltpu.VMEM((chunks, size, width), bf16),
+            pltpu.VMEM((chunks, size, width), bf16),
+            pltpu.VMEM((chunks, 2 * (width // size), size), f32),
+            pltpu.VMEM((chunks, 2 * (width // size), size), f32),
+            pltpu.VMEM((2, tokens, 2 * size), f32),
+            pltpu.VMEM((2, tokens, size), f32),
+            pltpu.VMEM((8, size), f32),
+            pltpu.VMEM((tokens, size), bf16),
+            dma((3,)), dma((3,)), dma((3,)), dma((chunks,)), dma((chunks,)),
+            dma((2, chunks)), dma((2, chunks)), dma, dma,
+        ],
+        compiler_params=pltpu.CompilerParams(
+            collective_id=0, has_side_effects=True, vmem_limit_bytes=60 * 1024 * 1024),
+        name="favor_heads",
+    )(own_q, own_k, own_v, projections)
+    return jnp.transpose(out, (1, 0, 2))
+
+
+def pairs_fit(mesh, args):
+    queries, _, _, projections = args
+    seq, feat = mesh.shape["seq"], mesh.shape["feat"]
+    width = projections.shape[1] // feat
+    tokens, size = queries.shape[0] // seq, queries.shape[2]
+    return (seq == 4 and feat & (feat - 1) == 0 and queries.shape[1] == 2 * feat
+            and size == 128 and width % size == 0 and tokens % 16 == 0)
+
+
 def solution(mesh):
     placed = (
         P("seq", None, None),
@@ -65,6 +339,11 @@
         P("seq", None, None),
         P(None, "feat", None),
     )
-    return jax.shard_map(
-        shards, mesh=mesh, in_specs=placed, out_specs=P("seq", "feat", None), check_vma=False
-    )
+
+    def run(*args):
+        body = functools.partial(paired_shards, mesh.shape["feat"]) if pairs_fit(mesh, args) else shards
+        return jax.shard_map(
+            body, mesh=mesh, in_specs=placed, out_specs=P("seq", "feat", None), check_vma=False
+        )(*args)
+
+    return run

time: 291 us -> 73.1 us (0.25)
  blocking collectives: 152 us -> 0 us
  matrix products: 64.3 us -> 0 us
  Pallas kernels: 0 us -> 62.2 us
  waiting for transfers between devices: 41.7 us -> 0 us
  other arithmetic: 14.5 us -> 0 us
  starting transfers between devices: 6.35 us -> 0 us
    psum x1 -> x0, blocking collectives: 142 us -> none  [shards(): key_state, key_mass = lax.psum((key_state, key_mass), 'seq')]
    dot_general x5 -> x0, matrix products: 64.3 us -> none  [the longest x1 18.6 us: partial_output(): jnp.einsum('thm,hm->th', query_phi.astype(jnp.float32), key_mass, precisi...]
    pallas_call x0 -> x1, Pallas kernels: none -> 62.2 us  [paired_shards(): pl.pallas_call(functools.partial(head_kernel, chunks, AHEAD, BEHIND, scal...]
    all_to_all x1 -> x0, waiting for transfers between devices: 41.7 us -> none  [shards(): lax.all_to_all(projections, 'feat', split_axis=0, concat_axis=1, tiled=True)]
    reduce_sum x2 -> x0, other arithmetic: 14.5 us -> none  [the longest x1 14.1 us: key_terms(): key_mass = jnp.sum(key_phi, axis=0, dtype=jnp.float32)]
    pmax x1 -> x0, blocking collectives: 10.2 us -> none  [shards(): key_peak = lax.pmax(jnp.max(key_expo, axis=(0, 2)), 'seq')]
    all_to_all x1 -> x0, starting transfers between devices: 6.35 us -> none  [shards(): lax.all_to_all(projections, 'feat', split_axis=0, concat_axis=1, tiled=True)]
    dynamic_slice x3 -> x2, local copies, waits for them, and re-layouts: 6.94 us -> 5.2 us  [paired_shards(): lax.dynamic_slice_in_dim(a, start, 2, 1)]
  transfers between devices with their start and end apart: 1 -> 0, of which waited for: 1 -> 0; matrix products, arithmetic and copies ran while one was open for 3% -> 0% of each run, Pallas kernels for 0% -> 0%
where the time goes in v1:
time: 73.1 us; the launch traced here: 72.9 us
  Pallas kernels  62.2 us (85%)
  local copies, waits for them, and re-layouts  10.7 us (15%)
    pallas_call x1, Pallas kernels, paired_shards(): pl.pallas_call(functools.partial(head_kernel, chunks, AHEAD, BEHIND, scal...  62.2 us
    dynamic_slice x2, local copies, waits for them, and re-layouts, paired_shards(): lax.dynamic_slice_in_dim(a, start, 2, 1)  5.2 us
    unnamed x3, local copies, waits for them, and re-layouts  3.16 us
    transpose x1, local copies, waits for them, and re-layouts, paired_shards(): return jnp.transpose(out, (1, 0, 2))  2.31 us

profile of v1, /device:TPU:0, one launch (start us, length us, event | category | flops | bytes accessed | tf_op | source)
XLA Modules:
  0.0 72.9 jit_solution(5369023605784921137)
XLA Ops:
  0.0 2.1 %constant_dynamic-slice_fusion.2 = bf16[960,2,128]{2,1,0:T(2,128)(2,1)S(1)} fusion(bf16[960,16,128]{2,1,0:T(8,128)(2,1)} %param.4, s32[]{:T(128)S(6)} %select_n.2), kind=kLoop, calls=%fused_computation.4 | loop fusion | bytes 983044 | tf_op jit(solution)/shard_map/dynamic_slice | solution.py:290
  2.1 0.8 %copy.15 = bf16[960,2,128]{2,0,1:T(8,128)(2,1)} copy(bf16[960,2,128]{2,1,0:T(2,128)(2,1)S(1)} %constant_dynamic-slice_fusion.2) | data formatting | bytes 983040
  2.9 3.1 %constant_dynamic-slice_fusion = (bf16[960,2,128]{2,1,0:T(2,128)(2,1)S(1)}, bf16[960,2,128]{2,1,0:T(2,128)(2,1)S(1)}) fusion(bf16[960,16,128]{2,1,0:T(8,128)(2,1)} %param.6, s32[]{:T(128)S(6)} %select_n.2, bf16[960,16,128]{2,1,0:T(8,128)(2,1)} %param.5), kind=kLoop, calls=%fused_computation.2 | loop fusion | bytes 1966084 | tf_op jit(solution)/shard_map/dynamic_slice | solution.py:290
  6.1 1.4 %copy.11 = bf16[960,2,128]{0,2,1:T(8,128)(2,1)} copy(bf16[960,2,128]{2,1,0:T(2,128)(2,1)S(1)} %get-tuple-element.5) | data formatting | bytes 983040
  7.5 0.9 %copy.14 = bf16[960,2,128]{2,0,1:T(8,128)(2,1)} copy(bf16[960,2,128]{2,1,0:T(2,128)(2,1)S(1)} %get-tuple-element.6) | data formatting | bytes 983040
  8.4 62.2 %favor_heads.1 = bf16[2,960,128]{2,1,0:T(8,128)(2,1)} custom-call(bf16[2,960,128]{2,1,0:T(8,128)(2,1)} %bitcast.9, bf16[2,960,128]{2,1,0:T(8,128)(2,1)} %bitcast.10, bf16[2,128,960]{2,1,0:T(8,128)(2,1)} %bitcast.8, bf16[16,512,128]{2,1,0:T(8,128)(2,1)} %dirs_hbm.1), custom_call_target="tpu_custom_call" | custom-call | tf_op jit(solution)/shard_map/favor_heads/pallas_call | solution.py:295
  70.6 2.3 %copy.8 = bf16[960,2,128]{2,1,0:T(2,128)(2,1)} copy(bf16[960,2,128]{2,0,1:T(8,128)(2,1)} %bitcast.11) | data formatting | bytes 983040 | tf_op jit(solution)/shard_map/transpose | solution.py:323

commit v2 on v1

--- a/solution.py
+++ b/solution.py
@@ -9,8 +9,9 @@
 from jax.sharding import PartitionSpec as P
 
 E = 128
-AHEAD = 2
-BEHIND = 1
+AHEAD = 1
+BEHIND = 3
+LATE = 2
 
 
 def key_exponents(key_vectors, directions, scaling):
@@ -84,11 +85,11 @@
 
 
 def head_kernel(
-    chunks, ahead, behind, scale,
+    chunks, ahead, behind, late, scale,
     q_hbm, k_hbm, v_hbm, dirs_hbm, out_ref,
     q_ref, k_ref, v_ref, diag_ref, w_ref,
     state_ref, peak_ref, send_ref, recv_ref, send_aux, recv_aux,
-    acc_ref, row_ref, top_ref, result_ref,
+    acc_ref, row_ref, top_ref, drop_ref, table_ref, result_ref,
     load_sem, x_send, x_recv, w_send, w_recv, y_send, y_recv, o_send, o_recv,
 ):
     tokens, size = k_ref.shape[1:]
@@ -96,9 +97,12 @@
     groups = width // size
     seq = lax.axis_index("seq")
     feat = lax.axis_index("feat")
-    side = seq % 2
-    x_mate = flip(seq, 1, 4)
-    y_mate = flip(seq, 2, 4)
+    low, high = seq % 2, seq // 2
+    odd = feat % 2
+    side = low * (1 - odd) + high * odd
+    low_step, high_step = 1 - 2 * low, 2 - 4 * high
+    x_mate = seq + low_step * (1 - odd) + high_step * odd
+    y_mate = seq + low_step * odd + high_step * (1 - odd)
     mates = [flip(feat, bits, chunks) for bits in range(1, chunks)]
 
     own_loads = [
@@ -126,7 +130,7 @@
     w_copies = []
     for i, mate in enumerate(mates):
         w_copies.append(pltpu.make_async_remote_copy(
-            src_ref=dirs_hbm.at[mate * 2 + side], dst_ref=w_ref.at[i + 1],
+            src_ref=dirs_hbm.at[mate * 2 + low * (1 - mate % 2) + high * (mate % 2)], dst_ref=w_ref.at[i + 1],
             send_sem=w_send.at[i + 1], recv_sem=w_recv.at[i + 1],
             device_id={"feat": mate}, device_id_type=MESH))
     for copy in x_copies[:2] + w_copies + x_copies[2:]:
@@ -187,37 +191,34 @@
                 send_aux[slot, g:g + 1, :] = state[size:size + 1, cut]
                 send_aux[slot, groups + g:groups + g + 1, :] = peak[:, cut]
 
-    def query_unit(slot):
+    def combine(slot):
         own_peak = peak_ref[slot, 0:1, :]
         got_peak = jnp.concatenate([recv_aux[slot, groups + g:groups + g + 1, :] for g in range(groups)], axis=1)
         got_mass = jnp.concatenate([recv_aux[slot, g:g + 1, :] for g in range(groups)], axis=1)
         before = top_ref[0:1, 0:1]
         top = jnp.maximum(before, jnp.max(jnp.maximum(own_peak, got_peak), axis=1, keepdims=True))
         top_ref[...] = jnp.broadcast_to(top, top_ref.shape)
+        drop_ref[slot] = jnp.broadcast_to((before - top) * slope, drop_ref.shape[1:])
         own_gain = jnp.exp2((own_peak - top) * slope)
         got_gain = jnp.exp2((got_peak - top) * slope)
-        state = (state_ref[slot, 0:size, :] * own_gain + recv_ref[slot].astype(jnp.float32) * got_gain).astype(jnp.bfloat16)
+        state = state_ref[slot, 0:size, :] * own_gain + recv_ref[slot].astype(jnp.float32) * got_gain
         mass = state_ref[slot, size:size + 1, :] * own_gain + got_mass * got_gain
-        high = mass.astype(jnp.bfloat16).astype(jnp.float32)
-        table = jnp.concatenate([
-            state,
-            jnp.broadcast_to(high, (size // 2, width)).astype(jnp.bfloat16),
-            jnp.broadcast_to(mass - high, (size // 2, width)).astype(jnp.bfloat16)], axis=0)
-        drop = (before - top) * slope
-
-        def one_half(half, carry):
-            raw = dot_nt(q_ref[half], w_ref[slot])
-            last = row_ref[half]
-            peak = jnp.maximum(last, jnp.max(raw, axis=1, keepdims=True))
-            row_ref[half] = peak
-            wide = jnp.concatenate([peak] * groups, axis=1)
-            phi = jnp.exp2((raw - wide) * slope).astype(jnp.bfloat16)
-            part = dot_nt(phi, table)
-            fade = jnp.exp2((last - peak) * slope + drop)
-            acc_ref[half] = acc_ref[half] * jnp.concatenate([fade, fade], axis=1) + part
-            return carry
-
-        lax.fori_loop(0, 2, one_half, 0)
+        coarse = mass.astype(jnp.bfloat16).astype(jnp.float32)
+        table_ref[slot, 0:size, :] = state.astype(jnp.bfloat16)
+        half_shape = (size // 2, width)
+        table_ref[slot, size:size + size // 2, :] = jnp.broadcast_to(coarse, half_shape).astype(jnp.bfloat16)
+        table_ref[slot, size + size // 2:2 * size, :] = jnp.broadcast_to(mass - coarse, half_shape).astype(jnp.bfloat16)
+
+    def query_unit(half, slot):
+        raw = dot_nt(q_ref[half], w_ref[slot])
+        last = row_ref[half]
+        peak = jnp.maximum(last, jnp.max(raw, axis=1, keepdims=True))
+        row_ref[half] = peak
+        wide = jnp.concatenate([peak] * groups, axis=1)
+        phi = jnp.exp2((raw - wide) * slope).astype(jnp.bfloat16)
+        part = dot_nt(phi, table_ref[slot])
+        fade = jnp.exp2((last - peak) * slope + drop_ref[slot, 0:1, :])
+        acc_ref[half] = acc_ref[half] * jnp.concatenate([fade, fade], axis=1) + part
 
     def finish(half):
         numer = acc_ref[half, :, 0:size]
@@ -248,25 +249,32 @@
             own_loads[2].wait()
             x_copies[2].wait_recv()
 
-        @pl.when(t >= ahead + behind)
+        @pl.when((t >= ahead + behind) & (t < ahead + behind + chunks))
         def _():
             slot = t - ahead - behind
             for copy in state_copies(slot):
                 copy.wait_recv()
-            query_unit(slot)
+            combine(slot)
+            query_unit(1, slot)
+
+        @pl.when(t == ahead + behind + chunks - 1)
+        def _():
+            result_ref[...] = finish(1)
+            out_copy.start()
+
+        @pl.when(t >= ahead + behind + late)
+        def _():
+            query_unit(0, t - ahead - behind - late)
 
         return carry
 
+    out_copy = pltpu.make_async_remote_copy(
+        src_ref=result_ref, dst_ref=out_ref.at[side], send_sem=o_send, recv_sem=o_recv,
+        device_id={"seq": x_mate}, device_id_type=MESH)
     own_loads[0].wait()
     own_loads[1].wait()
     make_diag(0)
-    lax.fori_loop(0, chunks + ahead + behind, step, 0)
-
-    result_ref[...] = finish(1)
-    out_copy = pltpu.make_async_remote_copy(
-        src_ref=result_ref, dst_ref=out_ref.at[side], send_sem=o_send, recv_sem=o_recv,
-        device_id={"seq": x_mate}, device_id_type=MESH)
-    out_copy.start()
+    lax.fori_loop(0, chunks + ahead + behind + late, step, 0)
     out_ref[side] = finish(0)
     for copy in x_copies:
         copy.wait_send()
@@ -293,7 +301,7 @@
     bf16, f32 = jnp.bfloat16, jnp.float32
     dma = pltpu.SemaphoreType.DMA
     out = pl.pallas_call(
-        functools.partial(head_kernel, chunks, AHEAD, BEHIND, scale),
+        functools.partial(head_kernel, chunks, AHEAD, BEHIND, LATE, scale),
         out_shape=jax.ShapeDtypeStruct((2, tokens, size), bf16),
         in_specs=[pl.BlockSpec(memory_space=pl.ANY)] * 4,
         out_specs=pl.BlockSpec(memory_space=pltpu.VMEM),
@@ -312,6 +320,8 @@
             pltpu.VMEM((2, tokens, 2 * size), f32),
             pltpu.VMEM((2, tokens, size), f32),
             pltpu.VMEM((8, size), f32),
+            pltpu.VMEM((chunks, 8, size), f32),
+            pltpu.VMEM((chunks, 2 * size, width), bf16),
             pltpu.VMEM((tokens, size), bf16),
             dma((3,)), dma((3,)), dma((3,)), dma((chunks,)), dma((chunks,)),
             dma((2, chunks)), dma((2, chunks)), dma, dma,

time: 73.1 us -> 59.3 us (0.81)
  Pallas kernels: 62.2 us -> 48.4 us
    pallas_call x1, Pallas kernels: 62.2 us -> 48.4 us  [paired_shards(): pl.pallas_call(functools.partial(head_kernel, chunks, AHEAD, BEHIND, LATE...]
where the time goes in v2:
time: 59.3 us; the launch traced here: 59.1 us
  Pallas kernels  48.4 us (82%)
  local copies, waits for them, and re-layouts  10.7 us (18%)
    pallas_call x1, Pallas kernels, paired_shards(): pl.pallas_call(functools.partial(head_kernel, chunks, AHEAD, BEHIND, LATE...  48.4 us
    dynamic_slice x2, local copies, waits for them, and re-layouts, paired_shards(): lax.dynamic_slice_in_dim(a, start, 2, 1)  5.2 us
    unnamed x3, local copies, waits for them, and re-layouts  3.16 us
    transpose x1, local copies, waits for them, and re-layouts, paired_shards(): return jnp.transpose(out, (1, 0, 2))  2.31 us

profile of v2, /device:TPU:0, one launch (start us, length us, event | category | flops | bytes accessed | tf_op | source)
XLA Modules:
  0.0 59.1 jit_solution(8611807940681143828)
XLA Ops:
  0.0 2.1 %constant_dynamic-slice_fusion.2 = bf16[960,2,128]{2,1,0:T(2,128)(2,1)S(1)} fusion(bf16[960,16,128]{2,1,0:T(8,128)(2,1)} %param.4, s32[]{:T(128)S(6)} %select_n.2), kind=kLoop, calls=%fused_computation.4 | loop fusion | bytes 983044 | tf_op jit(solution)/shard_map/dynamic_slice | solution.py:298
  2.1 0.8 %copy.15 = bf16[960,2,128]{2,0,1:T(8,128)(2,1)} copy(bf16[960,2,128]{2,1,0:T(2,128)(2,1)S(1)} %constant_dynamic-slice_fusion.2) | data formatting | bytes 983040
  2.9 3.1 %constant_dynamic-slice_fusion = (bf16[960,2,128]{2,1,0:T(2,128)(2,1)S(1)}, bf16[960,2,128]{2,1,0:T(2,128)(2,1)S(1)}) fusion(bf16[960,16,128]{2,1,0:T(8,128)(2,1)} %param.6, s32[]{:T(128)S(6)} %select_n.2, bf16[960,16,128]{2,1,0:T(8,128)(2,1)} %param.5), kind=kLoop, calls=%fused_computation.2 | loop fusion | bytes 1966084 | tf_op jit(solution)/shard_map/dynamic_slice | solution.py:298
  6.1 1.4 %copy.11 = bf16[960,2,128]{0,2,1:T(8,128)(2,1)} copy(bf16[960,2,128]{2,1,0:T(2,128)(2,1)S(1)} %get-tuple-element.5) | data formatting | bytes 983040
  7.5 0.9 %copy.14 = bf16[960,2,128]{2,0,1:T(8,128)(2,1)} copy(bf16[960,2,128]{2,1,0:T(2,128)(2,1)S(1)} %get-tuple-element.6) | data formatting | bytes 983040
  8.4 48.4 %favor_heads.1 = bf16[2,960,128]{2,1,0:T(8,128)(2,1)} custom-call(bf16[2,960,128]{2,1,0:T(8,128)(2,1)} %bitcast.9, bf16[2,960,128]{2,1,0:T(8,128)(2,1)} %bitcast.10, bf16[2,128,960]{2,1,0:T(8,128)(2,1)} %bitcast.8, bf16[16,512,128]{2,1,0:T(8,128)(2,1)} %dirs_hbm.1), custom_call_target="tpu_custom_call" | custom-call | tf_op jit(solution)/shard_map/favor_heads/pallas_call | solution.py:303
  56.8 2.3 %copy.8 = bf16[960,2,128]{2,1,0:T(2,128)(2,1)} copy(bf16[960,2,128]{2,0,1:T(8,128)(2,1)} %bitcast.11) | data formatting | bytes 983040 | tf_op jit(solution)/shard_map/transpose | solution.py:333

commit v3 on v2

--- a/solution.py
+++ b/solution.py
@@ -11,7 +11,7 @@
 E = 128
 AHEAD = 1
 BEHIND = 3
-LATE = 2
+LATE = 3
 
 
 def key_exponents(key_vectors, directions, scaling):

time: 59.3 us -> 58.5 us (0.987)
  Pallas kernels: 48.4 us -> 47.6 us
    pallas_call x1, Pallas kernels: 48.4 us -> 47.6 us  [paired_shards(): pl.pallas_call(functools.partial(head_kernel, chunks, AHEAD, BEHIND, LATE...]
where the time goes in v3:
time: 58.5 us; the launch traced here: 58.3 us
  Pallas kernels  47.6 us (81%)
  local copies, waits for them, and re-layouts  10.7 us (18%)
    pallas_call x1, Pallas kernels, paired_shards(): pl.pallas_call(functools.partial(head_kernel, chunks, AHEAD, BEHIND, LATE...  47.6 us
    dynamic_slice x2, local copies, waits for them, and re-layouts, paired_shards(): lax.dynamic_slice_in_dim(a, start, 2, 1)  5.2 us
    unnamed x3, local copies, waits for them, and re-layouts  3.16 us
    transpose x1, local copies, waits for them, and re-layouts, paired_shards(): return jnp.transpose(out, (1, 0, 2))  2.31 us

profile of v3, /device:TPU:0, one launch (start us, length us, event | category | flops | bytes accessed | tf_op | source)
XLA Modules:
  0.0 58.3 jit_solution(5277050540024168156)
XLA Ops:
  0.0 2.1 %constant_dynamic-slice_fusion.2 = bf16[960,2,128]{2,1,0:T(2,128)(2,1)S(1)} fusion(bf16[960,16,128]{2,1,0:T(8,128)(2,1)} %param.4, s32[]{:T(128)S(6)} %select_n.2), kind=kLoop, calls=%fused_computation.4 | loop fusion | bytes 983044 | tf_op jit(solution)/shard_map/dynamic_slice | solution.py:298
  2.1 0.8 %copy.15 = bf16[960,2,128]{2,0,1:T(8,128)(2,1)} copy(bf16[960,2,128]{2,1,0:T(2,128)(2,1)S(1)} %constant_dynamic-slice_fusion.2) | data formatting | bytes 983040
  2.9 3.1 %constant_dynamic-slice_fusion = (bf16[960,2,128]{2,1,0:T(2,128)(2,1)S(1)}, bf16[960,2,128]{2,1,0:T(2,128)(2,1)S(1)}) fusion(bf16[960,16,128]{2,1,0:T(8,128)(2,1)} %param.6, s32[]{:T(128)S(6)} %select_n.2, bf16[960,16,128]{2,1,0:T(8,128)(2,1)} %param.5), kind=kLoop, calls=%fused_computation.2 | loop fusion | bytes 1966084 | tf_op jit(solution)/shard_map/dynamic_slice | solution.py:298
  6.1 1.4 %copy.11 = bf16[960,2,128]{0,2,1:T(8,128)(2,1)} copy(bf16[960,2,128]{2,1,0:T(2,128)(2,1)S(1)} %get-tuple-element.5) | data formatting | bytes 983040
  7.5 0.9 %copy.14 = bf16[960,2,128]{2,0,1:T(8,128)(2,1)} copy(bf16[960,2,128]{2,1,0:T(2,128)(2,1)S(1)} %get-tuple-element.6) | data formatting | bytes 983040
  8.4 47.6 %favor_heads.1 = bf16[2,960,128]{2,1,0:T(8,128)(2,1)} custom-call(bf16[2,960,128]{2,1,0:T(8,128)(2,1)} %bitcast.9, bf16[2,960,128]{2,1,0:T(8,128)(2,1)} %bitcast.10, bf16[2,128,960]{2,1,0:T(8,128)(2,1)} %bitcast.8, bf16[16,512,128]{2,1,0:T(8,128)(2,1)} %dirs_hbm.1), custom_call_target="tpu_custom_call" | custom-call | tf_op jit(solution)/shard_map/favor_heads/pallas_call | solution.py:303
  56.0 2.3 %copy.8 = bf16[960,2,128]{2,1,0:T(2,128)(2,1)} copy(bf16[960,2,128]{2,0,1:T(8,128)(2,1)} %bitcast.11) | data formatting | bytes 983040 | tf_op jit(solution)/shard_map/transpose | solution.py:333
